TPU v7x, 32 devices: a whole 2x2x4 slice. The times are simulated.
32 devices in a mesh: dp: 4 (over x, core), expert: 8 (over z, y).
Axes of the slice: x: 2, y: 2, z: 4, core: 2. Of those that a mesh axis runs over, the one named last changes fastest.
Arguments:
- grad_partials: bfloat16 [4, 7168, 8192], P('dp', None, 'expert'), may hold values from -6 to 6
- master_weights: float32 [7168, 8192], P('dp', 'expert'), may hold values from -0.3125 to 0.3125
- first_moment: float32 [7168, 8192], P('dp', 'expert'), may hold values from -2 to 2
- second_moment: float32 [7168, 8192], P('dp', 'expert'), may hold values from 0.02 to 0.5
- resident_weights: bfloat16 [7168, 16384], P('dp', 'expert'), may hold values from -0.6 to 0.6
- token_tiles: bfloat16 [8192, 7168], P('expert', 'dp'), may hold values from -6 to 6
- owner_expert: int32 [8], replicated, may hold values from 0 to 3, as said below
- live_rows: int32 [8], P('expert'), may hold values from 256 to 1024, as said below
Outputs:
- updated_master: float32 [7168, 8192], P('dp', 'expert')
- projected: bfloat16 [8192, 2048], P('expert', 'dp')
Inputs may be any that keep to these rules, and one draw needn't show every extreme that they name: `owner_expert`: each owner hosts one of the 4 experts; every expert is hosted by at least one owner, some by several. The first live_rows[o] of owner o's rows are live; some owner has all 1024 rows live.
All inputs are finite; a program needn't handle non-finite values.
Results may differ from a plain program's by a relative error of at most 0.035.
Values may be sent and summed in bfloat16 or wider, within the bound.
No kernel may reach another device: no remote copies, remote signals or barrier semaphores. Data moves between devices by JAX's collectives and lax.ppermute only.
A program may use at most 192 MiB of HBM per device.

v0:
```python
import jax
import jax.numpy as jnp
from jax import lax
from jax.sharding import PartitionSpec as P

EXPERTS = 4
QB = 128
beta_first = 0.9
beta_second = 0.95
learn_rate = 0.02
decay_rate = 0.1
adam_epsilon = 1e-08
scale_epsilon = 1e-06
quant_range = 448.0
grid_step = 8.0
bias_first = 1.0 - 0.9**20
bias_second = 1.0 - 0.95**20


def adamw(gradient, master_weights, first_moment, second_moment):
    moment_one = beta_first * first_moment + (1.0 - beta_first) * gradient
    moment_two = beta_second * second_moment + (1.0 - beta_second) * gradient * gradient
    update = moment_one / bias_first / (jnp.sqrt(moment_two / bias_second) + adam_epsilon)
    return master_weights - learn_rate * (update + decay_rate * master_weights)


def block_product(stacked, weight):
    depth_blocks = stacked.shape[0]
    width_total = weight.shape[1]
    blocks = weight.reshape(depth_blocks, QB, width_total // QB, QB)
    largest = jnp.max(jnp.abs(blocks), axis=(1, 3))
    scales = (largest + scale_epsilon) / quant_range
    ratio = blocks / scales[:, None, :, None]
    level = grid_step * jnp.floor(ratio / grid_step + 0.5)
    quantized = level.astype(jnp.bfloat16).reshape(depth_blocks, QB, width_total)
    col_scales = jnp.repeat(scales, QB, axis=1)

    def step_block(running, inputs):
        tile_part, weight_part, scale_part = inputs
        product = jnp.dot(tile_part, weight_part, preferred_element_type=jnp.float32)
        return (running + product * scale_part[None, :], None)

    initial = jnp.zeros((stacked.shape[1], width_total), jnp.float32)
    result, unused = lax.scan(step_block, initial, (stacked, quantized, col_scales))
    return result


def body(
    grad_partials,
    master_weights,
    first_moment,
    second_moment,
    resident_weights,
    token_tiles,
    owner_expert,
    live_rows,
):
    gradient = lax.psum_scatter(
        grad_partials[0].astype(jnp.float32).astype(jnp.bfloat16),
        "dp",
        scatter_dimension=0,
        tiled=True,
    ).astype(jnp.float32)
    updated_master = adamw(gradient, master_weights, first_moment, second_moment)
    delta = (updated_master - master_weights).astype(jnp.bfloat16)
    group_size = lax.axis_size("expert") // EXPERTS
    own_index = lax.axis_index("expert")
    own_expert = owner_expert[own_index]
    rows_local = token_tiles.shape[0]
    depth_blocks = token_tiles.shape[1] // QB
    stacked = token_tiles.reshape(rows_local, depth_blocks, QB).transpose(1, 0, 2)
    part_cols = delta.shape[1]
    gathered = lax.all_gather(delta[None], "expert", axis=0, tiled=True)
    own_pieces = lax.dynamic_slice_in_dim(gathered, own_expert * group_size, group_size, 0)
    change = own_pieces.transpose(1, 0, 2).reshape(own_pieces.shape[1], group_size * part_cols)
    weight = resident_weights.astype(jnp.float32) + change.astype(jnp.float32)
    partial_out = block_product(stacked, weight)
    summed = lax.psum_scatter(
        partial_out.astype(jnp.bfloat16), "dp", scatter_dimension=1, tiled=True
    ).astype(jnp.float32)
    row_index = lax.broadcasted_iota(jnp.int32, summed.shape, 0)
    projected = jnp.where(row_index < live_rows[0], summed, jnp.float32(0.0)).astype(jnp.bfloat16)
    return (updated_master, projected)


def solution(mesh):
    placed = (
        P("dp", None, "expert"),
        P("dp", "expert"),
        P("dp", "expert"),
        P("dp", "expert"),
        P("dp", "expert"),
        P("expert", "dp"),
        P(),
        P("expert"),
    )
    return jax.shard_map(
        body,
        mesh=mesh,
        in_specs=placed,
        out_specs=(P("dp", "expert"), P("expert", "dp")),
        check_vma=False,
    )
```

profile of v0, /device:TPU:0, one launch (start us, length us, event | category | flops | bytes accessed | tf_op | source)
XLA Modules:
  0.0 945.2 jit_solution(4258799347159159431)
XLA Ops:
  7.2 0.0 reduce-scatter.3.cloned.1.call-start
  7.2 0.7 reduce-scatter.3.cloned.1.call-update
  7.9 0.0 copy-start
  7.9 0.0 all-gather.3.cloned.1.call-start
  8.0 119.3 %reduce-scatter.3.cloned.1.call-done = bf16[1792,1024]{1,0:T(8,128)(2,1)} async-done(((bf16[7168,1024]{1,0:T(8,128)(2,1)}), bf16[1792,1024]{1,0:T(8,128)(2,1)}) %reduce-scatter.3.cloned.1.call-update) | async-done | bytes 3670032 | tf_op jit(solution)/shard_map/reduce_scatter | solution.py:58
  127.3 14.3 %subtract_convert_fusion = (bf16[1792,1024]{1,0:T(8,128)(2,1)}, f32[1792,1024]{1,0:T(8,128)}) fusion(f32[1792,1024]{1,0:T(8,128)} %param.11, f32[1792,1024]{1,0:T(8,128)} %param.13, bf16[1792,1024]{1,0:T(8,128)(2,1)} %reduce-scatter.3.cloned.1.call-done, f32[1792,1024]{1,0:T(8,128)} %param.12), kind=kLoop, calls=%fused_computation.24 | loop fusion | flops 33030144 | bytes 36700160 | tf_op jit(solution)/shard_map/convert_element_type | solution.py:65
  141.6 0.0 all-gather.3.cloned.1.call-update
  141.6 0.0 reduce-scatter.5.cloned.1.call-start
  141.6 0.0 copy-done
  141.6 0.6 dynamic_slice.18
  142.9 6.1 copy.11
  149.0 551.7 %all-gather.3.cloned.1.call-done = bf16[14336,1024]{1,0:T(8,128)(2,1)} async-done(((bf16[1792,1024]{1,0:T(8,128)(2,1)}), bf16[14336,1024]{1,0:T(8,128)(2,1)}) %all-gather.3.cloned.1.call-update) | async-done | bytes 29360144 | tf_op jit(solution)/shard_map/all_gather | solution.py:73
  700.8 10.1 %convert_bitcast_fusion = f32[2,224,8,1024]{3,2,1,0:T(8,128)} fusion(bf16[8,1792,1024]{2,1,0:T(8,128)(2,1)} %bitcast.41, s32[]{:T(128)S(6)} %select_n.11), kind=kLoop, calls=%fused_computation.8 | loop fusion | flops 3670016 | bytes 22020100
  710.9 13.6 %copy.15 = f32[2,224,8,1024]{3,2,0,1:T(8,128)} copy(f32[2,224,8,1024]{3,2,1,0:T(8,128)} %convert_bitcast_fusion) | data formatting | bytes 29360128 | tf_op jit(solution)/shard_map/convert_element_type | solution.py:76
  724.5 18.8 %abs_bitcast_fusion = (f32[224,8,16,128]{3,1,2,0:T(8,128)}, f32[1792,2048]{1,0:T(8,128)}) fusion(f32[1792,2048]{1,0:T(8,128)} %bitcast.37, bf16[1792,2048]{1,0:T(8,128)(2,1)} %param.14), kind=kLoop, calls=%fused_computation.10 | loop fusion | flops 11010048 | bytes 51380224
  743.3 14.0 %copy.16 = f32[224,8,16,128]{3,2,1,0:T(8,128)} copy(f32[224,8,16,128]{3,1,2,0:T(8,128)} %get-tuple-element.63) | data formatting | bytes 29360128
  757.2 6.0 bitcast_reduce_fusion
  763.2 0.1 div.44
  763.4 9.1 multiply_convert_fusion
  772.5 113.2 %while.11 = (s32[]{:T(128)}, f32[1024,2048]{1,0:T(8,128)}, bf16[14,1024,128]{1,2,0:T(8,128)(2,1)}, bf16[14,128,2048]{2,1,0:T(8,128)(2,1)}, f32[14,2048]{1,0:T(8,128)S(1)}, /*index=5*/s32[]{:T(128)}, s32[]{:T(128)}) while((s32[]{:T(128)}, f32[1024,2048]{1,0:T(8,128)}, bf16[14,1024,128]{1,2,0:T(8,128)(2,1)}, ...), condition=%wide.region_3.4_spmd.clone, body=%wide.region_2.3_spmd.clone.sunk | while | flops 543162368 | bytes 17589336 | solution.py:44
  772.5 5.7 select_add_fusion.2
  778.3 8.2 select_add_fusion.2
  786.5 8.2 select_add_fusion.2
  794.8 8.2 select_add_fusion.2
  803.1 8.2 select_add_fusion.2
  811.3 8.2 select_add_fusion.2
  819.6 8.2 select_add_fusion.2
  827.8 8.2 select_add_fusion.2
  836.1 8.2 select_add_fusion.2
  844.4 8.2 select_add_fusion.2
  852.6 8.2 select_add_fusion.2
  860.9 8.2 select_add_fusion.2
  869.2 8.2 select_add_fusion.2
  877.4 8.2 select_add_fusion.2
  885.7 6.0 convert_element_type.40
  891.6 0.0 reduce-scatter.5.cloned.1.call-update
  892.3 43.9 %reduce-scatter.5.cloned.1.call-done = bf16[1024,512]{1,0:T(8,128)(2,1)} async-done(((bf16[1024,2048]{1,0:T(8,128)(2,1)}), bf16[1024,512]{1,0:T(8,128)(2,1)}) %reduce-scatter.5.cloned.1.call-update) | async-done | bytes 1048592 | tf_op jit(solution)/shard_map/reduce_scatter | solution.py:78
  936.2 2.5 select_convert_fusion
  (19 shorter events, 0.2 us)
Async XLA Ops:
  7.2 120.1 %reduce-scatter.3.cloned.1.call-start = ((), (), s32[]{:S(2)}) async-start(), calls=%async_computation.2 | async-start | bytes 18350080 | tf_op jit(solution)/shard_map/reduce_scatter | solution.py:58
  7.9 133.7 %copy-start = (s32[8]{0:T(128)S(1)}, s32[8]{0:T(128)}, u32[]{:S(2)}) copy-start(s32[8]{0:T(128)} %param.16) | copy-start | bytes 100
  7.9 692.8 %all-gather.3.cloned.1.call-start = ((), (), s32[]{:S(2)}) async-start(), calls=%async_computation.4 | async-start | bytes 33030144 | tf_op jit(solution)/shard_map/all_gather | solution.py:73
  141.6 794.6 %reduce-scatter.5.cloned.1.call-start = ((), (), s32[]{:S(2)}) async-start(), calls=%async_computation.3 | async-start | bytes 5242880 | tf_op jit(solution)/shard_map/reduce_scatter | solution.py:78
Sparse Core Ops, SparseCore 0:
  10.6 116.6 reduce-scatter.2
  141.7 559.0 all-gather.2
  891.8 44.3 reduce-scatter.4
where the time goes:
time: 946 us; the launch traced here: 945 us
  waiting for transfers between devices  716 us (76%)
  matrix products  113 us (12%)
  other arithmetic  66.7 us (7%)
  local copies, waits for them, and re-layouts  34.6 us (4%)
  between operations  15.1 us (2%)
    all_gather x1, waiting for transfers between devices, body(): gathered = lax.all_gather(delta[None], 'expert', axis=0, tiled=True)  552 us
    reduce_scatter x1, waiting for transfers between devices, body(): lax.psum_scatter(grad_partials[0].astype(jnp.float32).astype(jnp.bfloat16...  119 us
    dot_general x14, matrix products, step_block(): jnp.dot(tile_part, weight_part, preferred_element_type=jnp.float32)  113 us
    reduce_scatter x1, waiting for transfers between devices, body(): lax.psum_scatter(partial_out.astype(jnp.bfloat16), 'dp', scatter_dimensio...  43.9 us
    unnamed x3, other arithmetic  28.9 us
    unnamed x6, local copies, waits for them, and re-layouts  20.2 us
  transfers between devices with their start and end apart: 3, of which 3 were waited for; matrix products, arithmetic and copies ran while one was open for 1% of the time, Pallas kernels for 0%

commit v1 on v0

--- a/solution.py
+++ b/solution.py
@@ -70,7 +70,14 @@
     depth_blocks = token_tiles.shape[1] // QB
     stacked = token_tiles.reshape(rows_local, depth_blocks, QB).transpose(1, 0, 2)
     part_cols = delta.shape[1]
-    gathered = lax.all_gather(delta[None], "expert", axis=0, tiled=True)
+    ring = [delta[None]]
+    for hop in range(7):
+        ring.append(lax.ppermute(ring[-1], "expert", [(dev, (dev + 1) % 8) for dev in range(8)]))
+    gathered = jnp.roll(
+        jnp.concatenate(ring[::-1], axis=0),
+        (lax.axis_index("expert") + 1) * ring[0].shape[0],
+        axis=0,
+    )
     own_pieces = lax.dynamic_slice_in_dim(gathered, own_expert * group_size, group_size, 0)
     change = own_pieces.transpose(1, 0, 2).reshape(own_pieces.shape[1], group_size * part_cols)
     weight = resident_weights.astype(jnp.float32) + change.astype(jnp.float32)

time: 946 us -> 1020 us (1.078)
  local copies, waits for them, and re-layouts: 34.6 us -> 156 us
  waiting for transfers between devices: 716 us -> 668 us
    all_gather x1 -> x0, waiting for transfers between devices: 552 us -> none  [body(): gathered = lax.all_gather(delta[None], 'expert', axis=0, tiled=True)]
    ppermute x0 -> x7, waiting for transfers between devices: none -> 549 us  [body(): lax.ppermute(ring[-1], 'expert', [(dev, (dev + 1) % 8) for dev in range(8)])]
    unnamed x6 -> x55, local copies, waits for them, and re-layouts: 20.2 us -> 121 us
    reduce_scatter x1, waiting for transfers between devices: 119 us -> 86.4 us  [body(): lax.psum_scatter(grad_partials[0].astype(jnp.float32).astype(jnp.bfloat16...]
    unnamed x3 -> x2, other arithmetic: 28.9 us -> 0.01 us
    abs x0 -> x1, local copies, waits for them, and re-layouts: none -> 16.9 us  [block_product(): largest = jnp.max(jnp.abs(blocks), axis=(1, 3))]
    add x0 -> x1, local copies, waits for them, and re-layouts: none -> 15.3 us  [body(): weight = resident_weights.astype(jnp.float32) + change.astype(jnp.float32)]
    abs x0 -> x1, other arithmetic: none -> 14.6 us  [block_product(): largest = jnp.max(jnp.abs(blocks), axis=(1, 3))]
  transfers between devices with their start and end apart: 3 -> 9, of which waited for: 3 -> 9; matrix products, arithmetic and copies ran while one was open for 1% -> 5% of each run, Pallas kernels for 0% -> 0%
where the time goes in v1:
time: 1020 us
  waiting for transfers between devices  668 us (65%)
  local copies, waits for them, and re-layouts  156 us (15%)
  matrix products  114 us (11%)
  other arithmetic  62.5 us (6%)
  between operations  15.4 us (2%)
    ppermute x7, waiting for transfers between devices, body(): lax.ppermute(ring[-1], 'expert', [(dev, (dev + 1) % 8) for dev in range(8)])  549 us
    unnamed x55, local copies, waits for them, and re-layouts  121 us
    dot_general x14, matrix products, step_block(): jnp.dot(tile_part, weight_part, preferred_element_type=jnp.float32)  114 us
    reduce_scatter x1, waiting for transfers between devices, body(): lax.psum_scatter(grad_partials[0].astype(jnp.float32).astype(jnp.bfloat16...  86.4 us
    reduce_scatter x1, waiting for transfers between devices, body(): lax.psum_scatter(partial_out.astype(jnp.bfloat16), 'dp', scatter_dimensio...  32.8 us
  transfers between devices with their start and end apart: 9, of which 9 were waited for; matrix products, arithmetic and copies ran while one was open for 5% of the time, Pallas kernels for 0%

profile of v1, /device:TPU:0, one launch (start us, length us, event | category | flops | bytes accessed | tf_op | source)
XLA Modules:
  0.0 1017.6 jit_solution(6832132402945634980)
XLA Ops:
  7.2 18.5 %copy.22 = bf16[1,7168,1024]{1,2,0:T(8,128)(2,1)} copy(bf16[1,7168,1024]{2,1,0:T(8,128)(2,1)} %param.10) | data formatting | bytes 29360128 | tf_op args[0]
  25.8 8.4 copy.21
  34.2 9.4 copy.23
  43.6 8.6 copy.25
  52.3 86.4 %reduce-scatter.3.cloned.1.call-done = bf16[1792,1024]{0,1:T(8,128)(2,1)} async-done(((bf16[7168,1024]{0,1:T(8,128)(2,1)}), bf16[1792,1024]{0,1:T(8,128)(2,1)}) %reduce-scatter.3.cloned.1.call-update) | async-done | bytes 3670032 | tf_op jit(solution)/shard_map/reduce_scatter | solution.py:58
  138.7 13.7 %fusion.15 = (bf16[1,1792,1024]{1,2,0:T(8,128)(2,1)S(1)}, f32[1792,1024]{0,1:T(8,128)}) fusion(f32[1792,1024]{0,1:T(8,128)} %copy.25, f32[1792,1024]{0,1:T(8,128)} %copy.23, bf16[1792,1024]{0,1:T(8,128)(2,1)} %reduce-scatter.3.cloned.1.call-done, f32[1792,1024]{0,1:T(8,128)} %copy.21), kind=kLoop, calls=%fused_computation.23 | loop fusion | flops 33030144 | bytes 36700160 | tf_op jit(solution)/shard_map/broadcast_in_dim | solution.py:73
  155.6 82.1 %collective-permute-done = bf16[1,1792,1024]{1,2,0:T(8,128)(2,1)S(1)} collective-permute-done((bf16[1,1792,1024]{1,2,0:T(8,128)(2,1)S(1)}, bf16[1,1792,1024]{1,2,0:T(8,128)(2,1)S(1)}, u32[]{:S(2)}, u32[]{:S(2)}) %collective-permute-start) | collective-permute-done | bytes 3670048 | tf_op jit(solution)/shard_map/ppermute | solution.py:75
  239.6 82.7 %collective-permute-done.1 = bf16[1,1792,1024]{1,2,0:T(8,128)(2,1)S(1)} collective-permute-done((bf16[1,1792,1024]{1,2,0:T(8,128)(2,1)S(1)}, bf16[1,1792,1024]{1,2,0:T(8,128)(2,1)S(1)}, u32[]{:S(2)}, u32[]{:S(2)}) %collective-permute-start.1) | collective-permute-done | bytes 3670048 | tf_op jit(solution)/shard_map/ppermute | solution.py:75
  324.2 81.9 %collective-permute-done.2 = bf16[1,1792,1024]{1,2,0:T(8,128)(2,1)S(1)} collective-permute-done((bf16[1,1792,1024]{1,2,0:T(8,128)(2,1)S(1)}, bf16[1,1792,1024]{1,2,0:T(8,128)(2,1)S(1)}, u32[]{:S(2)}, u32[]{:S(2)}) %collective-permute-start.2) | collective-permute-done | bytes 3670048 | tf_op jit(solution)/shard_map/ppermute | solution.py:75
  407.8 81.0 %collective-permute-done.3 = bf16[1,1792,1024]{1,2,0:T(8,128)(2,1)S(1)} collective-permute-done((bf16[1,1792,1024]{1,2,0:T(8,128)(2,1)S(1)}, bf16[1,1792,1024]{1,2,0:T(8,128)(2,1)S(1)}, u32[]{:S(2)}, u32[]{:S(2)}) %collective-permute-start.3) | collective-permute-done | bytes 3670048 | tf_op jit(solution)/shard_map/ppermute | solution.py:75
  490.7 80.2 %collective-permute-done.4 = bf16[1,1792,1024]{1,2,0:T(8,128)(2,1)S(1)} collective-permute-done((bf16[1,1792,1024]{1,2,0:T(8,128)(2,1)S(1)}, bf16[1,1792,1024]{1,2,0:T(8,128)(2,1)S(1)}, u32[]{:S(2)}, u32[]{:S(2)}) %collective-permute-start.4) | collective-permute-done | bytes 3670048 | tf_op jit(solution)/shard_map/ppermute | solution.py:75
  572.6 79.4 %collective-permute-done.5 = bf16[1,1792,1024]{1,2,0:T(8,128)(2,1)} collective-permute-done((bf16[1,1792,1024]{1,2,0:T(8,128)(2,1)S(1)}, bf16[1,1792,1024]{1,2,0:T(8,128)(2,1)}, u32[]{:S(2)}, u32[]{:S(2)}) %collective-permute-start.5) | collective-permute-done | bytes 3670048 | tf_op jit(solution)/shard_map/ppermute | solution.py:75
  653.3 9.9 copy.27
  663.3 6.0 copy.26
  669.2 61.6 %collective-permute-done.6 = bf16[1,1792,1024]{1,2,0:T(8,128)(2,1)} collective-permute-done((bf16[1,1792,1024]{1,2,0:T(8,128)(2,1)}, bf16[1,1792,1024]{1,2,0:T(8,128)(2,1)}, u32[]{:S(2)}, u32[]{:S(2)}) %collective-permute-start.6) | collective-permute-done | bytes 3670048 | tf_op jit(solution)/shard_map/ppermute | solution.py:75
  730.8 4.1 constant_dynamic-update-slice_fusion.15
  734.9 4.3 constant_dynamic-update-slice_fusion.14
  739.1 2.2 constant_dynamic-update-slice_fusion.13
  741.3 2.1 constant_dynamic-update-slice_fusion.12
  752.4 4.0 constant_dynamic-update-slice_fusion.7
  756.5 4.1 constant_dynamic-update-slice_fusion.6
  764.7 2.2 constant_dynamic-update-slice_fusion.3
  768.9 2.1 constant_dynamic-update-slice_fusion.1
  773.1 9.9 dynamic-slice_convert_fusion
  783.0 14.6 %fusion.16 = (f32[1792,2048]{0,1:T(8,128)}, f32[1792,2048]{0,1:T(8,128)}) fusion(f32[2,1792,1024]{1,2,0:T(8,128)} %dynamic-slice_convert_fusion, bf16[1792,2048]{0,1:T(8,128)(2,1)S(1)} %bitcast.37), kind=kLoop, calls=%fused_computation.43 | loop fusion | flops 11010048 | bytes 51380224 | tf_op jit(solution)/shard_map/abs | solution.py:31
  797.6 16.9 %reshape.27 = f32[14,128,16,128]{1,0,3,2:T(8,128)} reshape(f32[1792,2048]{0,1:T(8,128)} %get-tuple-element.72) | data formatting | bytes 29360128 | tf_op jit(solution)/shard_map/abs | solution.py:31
  814.5 6.7 reduce_max.9
  821.6 15.3 %copy.29 = f32[1792,2048]{1,0:T(8,128)} copy(f32[1792,2048]{0,1:T(8,128)} %get-tuple-element.73) | data formatting | bytes 29360128 | tf_op jit(solution)/shard_map/add | solution.py:83
  836.8 9.0 multiply_convert_fusion
  845.9 114.2 %while.11 = (s32[]{:T(128)}, f32[1024,2048]{1,0:T(8,128)}, bf16[14,1024,128]{1,2,0:T(8,128)(2,1)}, bf16[14,128,2048]{2,1,0:T(8,128)(2,1)}, f32[14,2048]{1,0:T(8,128)S(1)}, /*index=5*/s32[]{:T(128)}, s32[]{:T(128)}) while((s32[]{:T(128)}, f32[1024,2048]{1,0:T(8,128)}, bf16[14,1024,128]{1,2,0:T(8,128)(2,1)}, ...), condition=%wide.region_3.4_spmd.clone, body=%wide.region_2.3_spmd.clone.sunk | while | flops 543162368 | bytes 17589336 | solution.py:44
  845.9 5.8 select_add_fusion.2
  851.7 8.3 select_add_fusion.2
  860.1 8.3 select_add_fusion.2
  868.4 8.3 select_add_fusion.2
  876.7 8.3 select_add_fusion.2
  885.1 8.3 select_add_fusion.2
  893.4 8.3 select_add_fusion.2
  901.8 8.3 select_add_fusion.2
  910.1 8.3 select_add_fusion.2
  918.4 8.3 select_add_fusion.2
  926.8 8.3 select_add_fusion.2
  935.1 8.3 select_add_fusion.2
  943.5 8.3 select_add_fusion.2
  951.8 8.3 select_add_fusion.2
  960.1 6.0 convert_element_type.40
  966.8 8.7 copy.32
  975.5 32.8 %reduce-scatter.5.cloned.1.call-done = bf16[1024,512]{1,0:T(8,128)(2,1)} async-done(((bf16[1024,2048]{1,0:T(8,128)(2,1)}), bf16[1024,512]{1,0:T(8,128)(2,1)}) %reduce-scatter.5.cloned.1.call-update) | async-done | bytes 1048592 | tf_op jit(solution)/shard_map/reduce_scatter | solution.py:85
  1008.3 2.5 select_convert_fusion
  (72 shorter events, 30.7 us)
Async XLA Ops:
  7.2 131.5 %reduce-scatter.3.cloned.1.call-start = ((), (), s32[]{:S(2)}) async-start(), calls=%async_computation.2 | async-start | bytes 18350080 | tf_op jit(solution)/shard_map/reduce_scatter | solution.py:58
  25.7 982.6 %reduce-scatter.5.cloned.1.call-start = ((), (), s32[]{:S(2)}) async-start(), calls=%async_computation.3 | async-start | bytes 5242880 | tf_op jit(solution)/shard_map/reduce_scatter | solution.py:85
  52.3 599.8 %copy-start.12 = (s32[8]{0:T(128)S(1)}, s32[8]{0:T(128)}, u32[]{:S(2)}) copy-start(s32[8]{0:T(128)} %param.16) | copy-start | bytes 100
  152.4 1.8 copy-start
  154.1 83.6 %collective-permute-start = (bf16[1,1792,1024]{1,2,0:T(8,128)(2,1)S(1)}, bf16[1,1792,1024]{1,2,0:T(8,128)(2,1)S(1)}, u32[]{:S(2)}, u32[]{:S(2)}) collective-permute-start(bf16[1,1792,1024]{1,2,0:T(8,128)(2,1)S(1)} %get-tuple-element.74), channel_id=1, source_target_pairs={{0,1},{1,2},{2,3},{3,4},{4,5},{5,6},{6,7},{7,0},{8,9},{9,10},{10,1... | collective-permute-start | bytes 11010056 | tf_op jit(solution)/shard_map/ppermute | solution.py:75
  237.7 1.9 copy-start.2
  239.6 82.7 %collective-permute-start.1 = (bf16[1,1792,1024]{1,2,0:T(8,128)(2,1)S(1)}, bf16[1,1792,1024]{1,2,0:T(8,128)(2,1)S(1)}, u32[]{:S(2)}, u32[]{:S(2)}) collective-permute-start(bf16[1,1792,1024]{1,2,0:T(8,128)(2,1)S(1)} %collective-permute-done), channel_id=1, source_target_pairs={{0,1},{1,2},{2,3},{3,4},{4,5},{5,6},{6,7},{7,0},{8,9},{9,10},{10,1... | collective-permute-start | bytes 11010056 | tf_op jit(solution)/shard_map/ppermute | solution.py:75
  322.4 1.8 copy-start.4
  324.2 81.9 %collective-permute-start.2 = (bf16[1,1792,1024]{1,2,0:T(8,128)(2,1)S(1)}, bf16[1,1792,1024]{1,2,0:T(8,128)(2,1)S(1)}, u32[]{:S(2)}, u32[]{:S(2)}) collective-permute-start(bf16[1,1792,1024]{1,2,0:T(8,128)(2,1)S(1)} %collective-permute-done.1), channel_id=1, source_target_pairs={{0,1},{1,2},{2,3},{3,4},{4,5},{5,6},{6,7},{7,0},{8,9},{9,10},{10,1... | collective-permute-start | bytes 11010056 | tf_op jit(solution)/shard_map/ppermute | solution.py:75
  406.1 1.8 copy-start.6
  407.8 81.0 %collective-permute-start.3 = (bf16[1,1792,1024]{1,2,0:T(8,128)(2,1)S(1)}, bf16[1,1792,1024]{1,2,0:T(8,128)(2,1)S(1)}, u32[]{:S(2)}, u32[]{:S(2)}) collective-permute-start(bf16[1,1792,1024]{1,2,0:T(8,128)(2,1)S(1)} %collective-permute-done.2), channel_id=1, source_target_pairs={{0,1},{1,2},{2,3},{3,4},{4,5},{5,6},{6,7},{7,0},{8,9},{9,10},{10,1... | collective-permute-start | bytes 11010056 | tf_op jit(solution)/shard_map/ppermute | solution.py:75
  488.9 1.8 copy-start.8
  490.7 80.2 %collective-permute-start.4 = (bf16[1,1792,1024]{1,2,0:T(8,128)(2,1)S(1)}, bf16[1,1792,1024]{1,2,0:T(8,128)(2,1)S(1)}, u32[]{:S(2)}, u32[]{:S(2)}) collective-permute-start(bf16[1,1792,1024]{1,2,0:T(8,128)(2,1)S(1)} %collective-permute-done.3), channel_id=1, source_target_pairs={{0,1},{1,2},{2,3},{3,4},{4,5},{5,6},{6,7},{7,0},{8,9},{9,10},{10,1... | collective-permute-start | bytes 11010056 | tf_op jit(solution)/shard_map/ppermute | solution.py:75
  570.8 1.8 copy-start.10
  572.6 79.4 %collective-permute-start.5 = (bf16[1,1792,1024]{1,2,0:T(8,128)(2,1)S(1)}, bf16[1,1792,1024]{1,2,0:T(8,128)(2,1)}, u32[]{:S(2)}, u32[]{:S(2)}) collective-permute-start(bf16[1,1792,1024]{1,2,0:T(8,128)(2,1)S(1)} %collective-permute-done.4), channel_id=1, source_target_pairs={{0,1},{1,2},{2,3},{3,4},{4,5},{5,6},{6,7},{7,0},{8,9},{9,10},{10,1... | collective-permute-start | bytes 11010056 | tf_op jit(solution)/shard_map/ppermute | solution.py:75
  652.0 78.8 %collective-permute-start.6 = (bf16[1,1792,1024]{1,2,0:T(8,128)(2,1)}, bf16[1,1792,1024]{1,2,0:T(8,128)(2,1)}, u32[]{:S(2)}, u32[]{:S(2)}) collective-permute-start(bf16[1,1792,1024]{1,2,0:T(8,128)(2,1)} %collective-permute-done.5), channel_id=1, source_target_pairs={{0,1},{1,2},{2,3},{3,4},{4,5},{5,6},{6,7},{7,0},{8,9},{9,10},{10,1... | collective-permute-start | bytes 11010056 | tf_op jit(solution)/shard_map/ppermute | solution.py:75
  669.2 69.9 %copy-start.11 = (bf16[1,1792,1024]{1,2,0:T(8,128)(2,1)S(1)}, bf16[1,1792,1024]{1,2,0:T(8,128)(2,1)}, u32[]{:S(2)}) copy-start(bf16[1,1792,1024]{1,2,0:T(8,128)(2,1)} %copy-done.10) | copy-start | bytes 11010052
  734.9 6.4 copy-start.9
  739.1 4.3 copy-start.7
  741.3 4.4 copy-start.5
  743.5 4.8 copy-start.3
  745.7 4.6 copy-start.1
  771.0 12.0 %slice-start = ((s8[7340032]{0:T(1024)(128)(4,1)}), s8[4194304]{0:T(1024)(128)(4,1)S(1)}, s32[]{:S(2)}) async-start(s8[7340032]{0:T(1024)(128)(4,1)} %bitcast.36), calls=%async_computation.4 | async-start | bytes 8388608
  773.1 9.9 slice-start.1
Sparse Core Ops, SparseCore 0:
  25.9 112.8 reduce-scatter.2
  966.3 41.9 reduce-scatter.4
